TPU v7x, 256 devices: a whole 4x4x8 slice. The times are simulated.
256 devices in a mesh: group: 8 (over z), tensor: 32 (over x, y, core).
Axes of the slice: x: 4, y: 4, z: 8, core: 2. Of those that a mesh axis runs over, the one named last changes fastest.
Arguments:
- residual_in: bfloat16 [8192, 2048], P(('group', 'tensor')), parts along dimension 0, may hold values from -22 to 22
- attn_gain: float32 [2048], replicated, may hold values from 0.5 to 1.5
- w_query: bfloat16 [2048, 4096], P(None, 'tensor'), may hold values from -0.125 to 0.125
- w_keyval: bfloat16 [1024, 2048], P('tensor'), may hold values from -0.125 to 0.125
- query_gain: float32 [128], replicated, may hold values from 0.1 to 1.9
- key_gain: float32 [128], replicated, may hold values from 0.1 to 1.9
- w_out: bfloat16 [4096, 2048], P('tensor'), may hold values from -0.09375 to 0.09375
- ffn_gain: float32 [2048], replicated, may hold values from 0.5 to 1.5
- w_gate: bfloat16 [32, 768, 2048], P('tensor'), may hold values from -0.125 to 0.125
- w_up: bfloat16 [32, 768, 2048], P('tensor'), may hold values from -0.125 to 0.125
- w_down: bfloat16 [32, 768, 2048], P('tensor'), may hold values from -0.21875 to 0.21875
- key_cache: bfloat16 [256, 1024, 512], P(('group', 'tensor')), parts along dimension 0, may hold values from -110 to 110
- value_cache: bfloat16 [256, 1024, 512], P(('group', 'tensor')), parts along dimension 0, may hold values from -18 to 18
- prefix_lens: int32 [256], P(('group', 'tensor')), parts along dimension 0, may hold values from 1 to 992
- accepted: int32 [256], P(('group', 'tensor')), parts along dimension 0, may hold values from 1 to 8
- accept_path: int32 [256, 8], P(('group', 'tensor')), parts along dimension 0, may hold values from 0 to 14, as said below
- parents: int32 [256, 32], P(('group', 'tensor')), parts along dimension 0, may hold values from -1 to 30, as said below
- slot_kinds: int32 [256], P(('group', 'tensor')), parts along dimension 0, may hold values from 0 to 1
- expert_ids: int32 [8192, 8], P('group'), parts along dimension 0, may hold values from 0 to 127, as said below
- gate_probs: float32 [8192, 8], P('group'), parts along dimension 0, may hold values from 0.1 to 1
Outputs:
- mixed: bfloat16 [8192, 2048], P(('group', 'tensor')), parts along dimension 0
There are 8 independent parts, one for each index of `group`. A program takes and returns all parts, laid end to end along the dimension named above; an argument that names none is the same for every part. Nothing has to cross between parts.
Inputs may be any that keep to these rules, and one draw needn't show every extreme that they name: `expert_ids`: the tokens of each slot name each of the 128 experts exactly 32 * 8 // 128 times; a token never names one expert twice. `accept_path`: each row starts at 0 and rises by 1 or 2 from one entry to the next. `parents`: node 0 of every slot has parent -1; every other node's parent is an earlier node of the same slot.
All inputs are finite; a program needn't handle non-finite values.
Results may differ from a plain program's by a relative error of at most 0.02.
Values may be sent and summed in bfloat16 or wider, within the bound.
A program may use at most 128 MiB of HBM per device.

v0:
```python
import math
import jax
import jax.numpy as jnp
from jax import lax
from jax.sharding import PartitionSpec as P

EXPERTS = 128
SINK = 4
WIN = 512
EPSILON = 1e-06
NEG_FILL = -1e30
ROPE_BASE = 1000000.0


def rms_rows(values, weight_gain):
    return (
        values
        * lax.rsqrt(jnp.mean(values * values, axis=-1, keepdims=True) + EPSILON)
        * weight_gain
    )


def rotate(values, angles):
    half_dim = values.shape[-1] // 2
    cosine = jnp.cos(angles)[:, None, :]
    sine_val = jnp.sin(angles)[:, None, :]
    lower_half = values[..., :half_dim]
    upper_half = values[..., half_dim:]
    return jnp.concatenate(
        [lower_half * cosine - upper_half * sine_val, upper_half * cosine + lower_half * sine_val],
        axis=-1,
    )


def ancestors(parent_row, count_new):
    parent_link = jax.nn.one_hot(parent_row, count_new, dtype=jnp.float32)
    reach_mat = jnp.eye(count_new, dtype=jnp.float32) + parent_link
    for unused in range((count_new - 1).bit_length()):
        reach_mat = jnp.minimum(jnp.dot(reach_mat, reach_mat, precision=lax.Precision.HIGHEST), 1.0)
    return reach_mat


def attend_parts(
    query_raw,
    keyval_raw,
    key_cache,
    value_cache,
    prefix_len,
    accepted_len,
    path_row,
    parent_row,
    kind_value,
    query_gain,
    key_gain,
):
    count_new = query_raw.shape[0]
    head_dim = query_gain.shape[0]
    kv_heads = key_cache.shape[-1] // head_dim
    q_heads = query_raw.shape[-1] // head_dim
    group_size = q_heads // kv_heads
    cache_len = key_cache.shape[0]
    acc_count = path_row.shape[0]
    total_len = prefix_len + accepted_len
    reach_mat = ancestors(parent_row, count_new)
    index_row = jnp.arange(count_new)
    causal = (index_row[None, :] <= index_row[:, None]).astype(jnp.float32)
    is_tree = kind_value == 1
    allowed = jnp.where(is_tree, reach_mat, causal) > 0.5
    depth_used = jnp.where(is_tree, jnp.sum(reach_mat, axis=1) - 1.0, index_row.astype(jnp.float32))
    position = total_len.astype(jnp.float32) + depth_used
    half_dim = head_dim // 2
    freq_table = jnp.exp(
        -(2.0 * jnp.arange(half_dim, dtype=jnp.float32) / head_dim) * math.log(ROPE_BASE)
    )
    angles = position[:, None] * freq_table[None, :]
    query_rot = rotate(
        rms_rows(query_raw.astype(jnp.float32).reshape(count_new, q_heads, head_dim), query_gain),
        angles,
    ).astype(jnp.bfloat16)
    key_width = kv_heads * head_dim
    key_new = rotate(
        rms_rows(
            keyval_raw[:, :key_width].astype(jnp.float32).reshape(count_new, kv_heads, head_dim),
            key_gain,
        ),
        angles,
    ).astype(jnp.bfloat16)
    value_new = keyval_raw[:, key_width:].reshape(count_new, kv_heads, head_dim)
    acc_rows = prefix_len + path_row
    key_acc = jnp.take(key_cache, acc_rows, axis=0).reshape(acc_count, kv_heads, head_dim)
    value_acc = jnp.take(value_cache, acc_rows, axis=0).reshape(acc_count, kv_heads, head_dim)
    key_old = key_cache.reshape(cache_len, kv_heads, head_dim)
    value_old = value_cache.reshape(cache_len, kv_heads, head_dim)
    cache_pos = jnp.arange(cache_len)
    seen_old = (cache_pos < prefix_len) & ((cache_pos < SINK) | (cache_pos >= total_len - WIN))
    acc_index = jnp.arange(acc_count)
    acc_pos = prefix_len + acc_index
    seen_acc = (acc_index < accepted_len) & ((acc_pos < SINK) | (acc_pos >= total_len - WIN))
    score_scale = head_dim ** (-0.5)
    query_group = query_rot.reshape(count_new, kv_heads, group_size, head_dim)
    score_old = (
        jnp.einsum("nkgd,mkd->kgnm", query_group, key_old, preferred_element_type=jnp.float32)
        * score_scale
    )
    score_acc = (
        jnp.einsum("nkgd,mkd->kgnm", query_group, key_acc, preferred_element_type=jnp.float32)
        * score_scale
    )
    score_new = (
        jnp.einsum("nkgd,mkd->kgnm", query_group, key_new, preferred_element_type=jnp.float32)
        * score_scale
    )
    score_old = jnp.where(seen_old[None, None, None, :], score_old, NEG_FILL)
    score_acc = jnp.where(seen_acc[None, None, None, :], score_acc, NEG_FILL)
    score_new = jnp.where(allowed[None, None], score_new, NEG_FILL)
    row_max = jnp.maximum(
        jnp.maximum(
            jnp.max(score_old, axis=-1, keepdims=True), jnp.max(score_acc, axis=-1, keepdims=True)
        ),
        jnp.max(score_new, axis=-1, keepdims=True),
    )
    expo_old = jnp.exp(score_old - row_max)
    expo_acc = jnp.exp(score_acc - row_max)
    expo_new = jnp.exp(score_new - row_max)
    denom_sum = (
        jnp.sum(expo_old, axis=-1, keepdims=True)
        + jnp.sum(expo_acc, axis=-1, keepdims=True)
        + jnp.sum(expo_new, axis=-1, keepdims=True)
    )
    probs_old = (expo_old / denom_sum).astype(jnp.bfloat16)
    probs_acc = (expo_acc / denom_sum).astype(jnp.bfloat16)
    probs_new = (expo_new / denom_sum).astype(jnp.bfloat16)
    result = jnp.einsum("kgnm,mkd->nkgd", probs_old, value_old, preferred_element_type=jnp.float32)
    result = result + jnp.einsum(
        "kgnm,mkd->nkgd", probs_acc, value_acc, preferred_element_type=jnp.float32
    )
    result = result + jnp.einsum(
        "kgnm,mkd->nkgd", probs_new, value_new, preferred_element_type=jnp.float32
    )
    return result.reshape(count_new, q_heads * head_dim).astype(jnp.bfloat16)


def route_rows(expert_ids, gate_probs, expert_names, count_rows):
    hit_mask = expert_ids[None, :, :] == expert_names[:, None, None]
    weights = jnp.sum(jnp.where(hit_mask, gate_probs[None], 0.0), axis=2)
    named_int = jnp.any(hit_mask, axis=2).astype(jnp.int32)
    chosen = jnp.argsort(1 - named_int, axis=1, stable=True)[:, :count_rows]
    return (chosen, jnp.take_along_axis(weights, chosen, axis=1))


def body(
    residual_in,
    attn_gain,
    w_query,
    w_keyval,
    query_gain,
    key_gain,
    w_out,
    ffn_gain,
    w_gate,
    w_up,
    w_down,
    key_cache,
    value_cache,
    prefix_lens,
    accepted,
    accept_path,
    parents,
    slot_kinds,
    expert_ids,
    gate_probs,
):
    devices = lax.axis_size("tensor")
    own_index = lax.axis_index("tensor")
    rows_here = residual_in.shape[0]
    model_width = residual_in.shape[1]
    slots_here = key_cache.shape[0]
    count_new = rows_here // slots_here
    row_start = own_index * rows_here
    normed_own = rms_rows(residual_in.astype(jnp.float32), attn_gain).astype(jnp.bfloat16)
    gathered = lax.all_gather(normed_own, "tensor", axis=0, tiled=True)
    query_part = jnp.dot(gathered, w_query, preferred_element_type=jnp.float32).astype(jnp.bfloat16)
    keyval_part = lax.dot_general(
        gathered, w_keyval, (((1,), (1,)), ((), ())), preferred_element_type=jnp.float32
    ).astype(jnp.bfloat16)
    query_tok, keyval_tok = (
        lax.all_to_all(query_part, "tensor", split_axis=0, concat_axis=1, tiled=True),
        lax.all_to_all(keyval_part, "tensor", split_axis=0, concat_axis=1, tiled=True),
    )

    def slot_attend(packed):
        return attend_parts(*packed, query_gain, key_gain)

    attn_own = lax.map(
        slot_attend,
        (
            query_tok.reshape(slots_here, count_new, -1),
            keyval_tok.reshape(slots_here, count_new, -1),
            key_cache,
            value_cache,
            prefix_lens,
            accepted,
            accept_path,
            parents,
            slot_kinds,
        ),
    )
    attn_own = attn_own.reshape(rows_here, -1)
    attn_heads = lax.all_to_all(attn_own, "tensor", split_axis=1, concat_axis=0, tiled=True)
    out_own = lax.psum_scatter(
        jnp.dot(attn_heads, w_out, preferred_element_type=jnp.float32).astype(jnp.bfloat16),
        "tensor",
        scatter_dimension=0,
        tiled=True,
    ).astype(jnp.float32)
    hidden_mid = residual_in.astype(jnp.float32) + out_own
    normed_ffn = rms_rows(hidden_mid, ffn_gain).astype(jnp.bfloat16)
    per_device = w_gate.shape[0]
    top_count = expert_ids.shape[1]
    all_names = jnp.arange(per_device * devices, dtype=jnp.int32)
    own_ids = lax.dynamic_slice_in_dim(expert_ids, row_start, rows_here, 0)
    own_gates = lax.dynamic_slice_in_dim(gate_probs, row_start, rows_here, 0)
    chosen, selected = route_rows(own_ids, own_gates, all_names, rows_here * top_count // EXPERTS)
    send_rows = normed_ffn[chosen]
    received = lax.all_to_all(send_rows, "tensor", split_axis=0, concat_axis=0, tiled=True)
    item_count = received.shape[1]
    grouped = received.reshape(devices, per_device, item_count, model_width)
    gate_val = jnp.einsum("spcd,pfd->spcf", grouped, w_gate, preferred_element_type=jnp.float32)
    up_val = jnp.einsum("spcd,pfd->spcf", grouped, w_up, preferred_element_type=jnp.float32)
    inner_act = (jax.nn.silu(gate_val) * up_val).astype(jnp.bfloat16)
    result = jnp.einsum("spcf,pfd->spcd", inner_act, w_down, preferred_element_type=jnp.float32)
    result = result.reshape(devices * per_device, item_count, model_width)
    returned = lax.all_to_all(
        result.astype(jnp.bfloat16), "tensor", split_axis=0, concat_axis=0, tiled=True
    ).astype(result.dtype)
    scaled = returned * selected[..., None]
    moe_own = (
        jnp.zeros((rows_here, model_width), jnp.float32)
        .at[chosen.reshape(-1)]
        .add(scaled.reshape(-1, model_width))
    )
    return (hidden_mid + moe_own).astype(jnp.bfloat16)


def solution(mesh):
    in_specs = (
        P(("group", "tensor"), None),
        P(),
        P(None, "tensor"),
        P("tensor", None),
        P(),
        P(),
        P("tensor", None),
        P(),
        P("tensor", None, None),
        P("tensor", None, None),
        P("tensor", None, None),
        P(("group", "tensor"), None, None),
        P(("group", "tensor"), None, None),
        P(("group", "tensor")),
        P(("group", "tensor")),
        P(("group", "tensor"), None),
        P(("group", "tensor"), None),
        P(("group", "tensor")),
        P("group", None),
        P("group", None),
    )
    out_specs = P(("group", "tensor"), None)
    return jax.shard_map(body, mesh=mesh, in_specs=in_specs, out_specs=out_specs, check_vma=False)
```

profile of v0, /device:TPU:1, one launch (start us, length us, event | category | flops | bytes accessed | tf_op | source)
XLA Modules:
  0.0 284.7 jit_solution(10480858248007846740)
XLA Ops:
  6.5 1.2 fusion.43
  7.7 1.7 fusion.45
  11.4 0.9 convolution_minimum_fusion.4
  13.1 0.7 copy.198
  13.8 2.2 reshape.276
  15.9 2.1 reshape.280
  18.7 2.5 gather_fusion.2
  21.2 2.5 gather_fusion.3
  24.3 0.7 multiply_cosine_fusion
  25.1 40.2 %all-gather.2.cloned.1.call-done = bf16[1024,2048]{1,0:T(8,128)(2,1)} async-done(((bf16[32,2048]{1,0:T(8,128)(2,1)}), bf16[1024,2048]{1,0:T(8,128)(2,1)}) %all-gather.2.cloned.1.call-update) | async-done | bytes 4194320 | tf_op jit(solution)/shard_map/all_gather | solution.py:181
  65.3 3.5 %convolution_convert_fusion.2 = bf16[1024,32]{0,1:T(8,128)(2,1)S(1)} fusion(bf16[1024,2048]{1,0:T(8,128)(2,1)} %all-gather.2.cloned.1.call-done, bf16[32,2048]{1,0:T(8,128)(2,1)S(1)} %copy-done.6), kind=kOutput, calls=%fused_computation.38 | convolution fusion | flops 134250496 | bytes 4390912 | tf_op jit(solution)/shard_map/dot_general | solution.py:183
  69.0 0.9 reshape.354
  69.8 5.3 %all-to-all-start.1 = ((bf16[32,2,512]{2,1,0:T(2,128)(2,1)}), bf16[32,2,512]{2,1,0:T(2,128)(2,1)S(1)}, u32[]{:S(2)}, u32[]{:S(2)}) async-start(bf16[32,2,512]{2,1,0:T(2,128)(2,1)} %reshape.354), calls=%async_computation.1 | async-start | bytes 131072 | tf_op jit(solution)/shard_map/all_to_all | solution.py:188
  75.1 4.3 %convolution_convert_fusion.1 = bf16[1024,128]{1,0:T(8,128)(2,1)} fusion(bf16[1024,2048]{1,0:T(8,128)(2,1)} %all-gather.2.cloned.1.call-done, bf16[2048,128]{1,0:T(8,128)(2,1)} %param.24), kind=kOutput, calls=%fused_computation.29 | convolution fusion | flops 537001984 | bytes 4980736 | tf_op jit(solution)/shard_map/dot_general | solution.py:182
  79.4 3.1 %all-to-all-done.1 = bf16[32,2,512]{2,1,0:T(2,128)(2,1)S(1)} async-done(((bf16[32,2,512]{2,1,0:T(2,128)(2,1)}), bf16[32,2,512]{2,1,0:T(2,128)(2,1)S(1)}, u32[]{:S(2)}, u32[]{:S(2)}) %all-to-all-start.1) | async-done | bytes 65568 | tf_op jit(solution)/shard_map/all_to_all | solution.py:188
  82.5 4.3 %all-to-all-start = ((bf16[32,32,128]{2,1,0:T(8,128)(2,1)}), bf16[32,32,128]{2,1,0:T(8,128)(2,1)S(1)}, u32[]{:S(2)}, u32[]{:S(2)}) async-start(bf16[32,32,128]{2,1,0:T(8,128)(2,1)} %bitcast.176), calls=%async_computation | async-start | bytes 524288 | tf_op jit(solution)/shard_map/all_to_all | solution.py:187
  86.8 0.9 reshape.355
  87.7 1.8 copy.200
  89.4 1.2 squeeze.37
  91.3 0.9 reshape.290
  92.2 0.7 multiply_reduce_fusion.1
  92.9 0.8 copy.201
  93.7 0.7 fusion.62
  94.5 1.4 reshape.282
  95.8 0.8 subtract_convert_fusion.1
  96.9 0.9 fusion.41
  97.8 0.9 fusion.46
  98.9 4.0 %bitcast_reduce_fusion = (f32[4,8,32]{1,2,0:T(8,128)S(1)}, f32[4,32,8,1024]{3,2,1,0:T(8,128)}) fusion(pred[1024]{0:T(1024)(128)(4,1)} %fusion.79, bf16[1024,4,128,1]{2,1,0,3:T(4,128)(2,1)} %bitcast.168, bf16[32,4,8,128]{3,2,1,0:T(8,128)(2,1)S(1)} %pad_maximum_fusion), kind=kOutput, calls=%fused_computation.6 | convolution fusion | flops 271580160 | bytes 5510144 | tf_op jit(solution)/shard_map/while/body/eval_jaxpr/nkgd,mkd->kgnm/dot_general | solution.py:102
  102.9 0.7 copy.197
  103.5 1.4 fusion.91
  104.9 1.2 fusion.92
  106.1 0.7 maximum_maximum_fusion
  107.0 3.2 %fusion.1 = f32[4,8,32]{1,2,0:T(8,128)S(1)} fusion(f32[4,32,8,1024]{3,2,1,0:T(8,128)} %get-tuple-element.67, f32[4,8,32]{1,2,0:T(8,128)S(1)} %copy.204, pred[1024]{0:T(1024)(128)(4,1)} %fusion.79), kind=kLoop, calls=%fused_computation.11 | loop fusion | flops 4193280 | bytes 4203520 | tf_op jit(solution)/shard_map/while/body/eval_jaxpr/reduce_sum | solution.py:126
  110.2 1.2 fusion.42
  111.4 1.2 divide_convert_fusion.4
  112.6 0.7 divide_convert_fusion.5
  113.3 0.8 copy.206
  114.1 0.9 copy.210
  115.0 1.0 copy.208
  116.0 3.7 %fusion.12 = f32[32,4,8,128]{3,2,0,1:T(8,128)S(1)} fusion(f32[4,32,8,1024]{3,2,1,0:T(8,128)} %get-tuple-element.67, f32[4,8,32]{1,2,0:T(8,128)S(1)} %copy.206, f32[4,8,32]{1,2,0:T(8,128)} %copy-done.4, pred[1024]{0:T(1024)(128)(4,1)} %fusion.79, bf16[1024,4,128,1]{2,1,0,3:T(4,128)(2,1)} %bitcast.174), kind=kOutput, calls=%fused_computation.20 | convolution fusion | flops 273678336 | bytes 5776384 | tf_op jit(solution)/shard_map/while/body/eval_jaxpr/kgnm,mkd->nkgd/dot_general | solution.py:133
  120.4 16.2 %all_to_all.55 = bf16[32,32,128]{2,0,1:T(8,128)(2,1)S(1)} all-to-all(bf16[32,32,128]{2,0,1:T(8,128)(2,1)S(1)} %copy.212), channel_id=1, replica_groups=mesh['group'=8,'tensor'=32] {'tensor'}, dimensions={1} | all-to-all | bytes 524288 | tf_op jit(solution)/shard_map/all_to_all | solution.py:209
  136.6 3.2 %convolution_convert_fusion = bf16[1024,2048]{1,0:T(8,128)(2,1)} fusion(bf16[1024,128]{1,0:T(8,128)(2,1)S(1)} %bitcast.169, bf16[128,2048]{1,0:T(8,128)(2,1)S(1)} %copy-done.3), kind=kOutput, calls=%fused_computation.10 | convolution fusion | flops 538968064 | bytes 4980736 | tf_op jit(solution)/shard_map/dot_general | solution.py:211
  139.8 0.8 constant_dynamic-slice_fusion.1
  140.7 0.8 sort.17
  142.3 83.0 %reduce-scatter.2.cloned.1.call-done = bf16[32,2048]{1,0:T(8,128)(2,1)} async-done(((bf16[1024,2048]{1,0:T(8,128)(2,1)}), bf16[32,2048]{1,0:T(8,128)(2,1)}) %reduce-scatter.2.cloned.1.call-update) | async-done | bytes 131088 | tf_op jit(solution)/shard_map/reduce_scatter | solution.py:210
  225.3 1.1 multiply_reduce_fusion
  226.4 1.1 multiply_convert_fusion
  227.4 1.4 gather_fusion
  228.9 1.8 reshape.308
  230.7 7.3 %all-to-all-start.3 = ((bf16[32,2,2048]{2,1,0:T(2,128)(2,1)}), bf16[32,2,2048]{2,1,0:T(2,128)(2,1)}, u32[]{:S(2)}, u32[]{:S(2)}) async-start(bf16[32,2,2048]{2,1,0:T(2,128)(2,1)} %reshape.308), calls=%async_computation.4 | async-start | bytes 524288 | tf_op jit(solution)/shard_map/all_to_all | solution.py:225
  238.0 0.7 bitcast_or_fusion
  238.9 0.8 constant_dynamic-slice_fusion
  239.7 0.8 gather_fusion.1
  240.7 6.3 %all-to-all-done.3 = bf16[32,2,2048]{2,1,0:T(2,128)(2,1)} async-done(((bf16[32,2,2048]{2,1,0:T(2,128)(2,1)}), bf16[32,2,2048]{2,1,0:T(2,128)(2,1)}, u32[]{:S(2)}, u32[]{:S(2)}) %all-to-all-start.3) | async-done | bytes 262176 | tf_op jit(solution)/shard_map/all_to_all | solution.py:225
  247.1 3.7 %fusion.18 = f32[32,1,2,768]{3,0,2,1:T(8,128)} fusion(bf16[1,768,2048]{2,1,0:T(8,128)(2,1)} %param.30, bf16[32,2,2048]{2,1,0:T(2,128)(2,1)} %all-to-all-done.3), kind=kOutput, calls=%fused_computation.30 | convolution fusion | flops 201326592 | bytes 3604480 | tf_op jit(solution)/shard_map/spcd,pfd->spcf/dot_general | solution.py:228
  250.8 4.8 %fusion.8 = bf16[32,2,2048]{2,0,1:T(8,128)(2,1)} fusion(bf16[1,768,2048]{2,1,0:T(8,128)(2,1)S(1)} %copy-done, bf16[1,768,2048]{2,1,0:T(8,128)(2,1)} %param.31, bf16[32,2,2048]{2,1,0:T(2,128)(2,1)} %all-to-all-done.3, f32[32,1,2,768]{3,0,2,1:T(8,128)} %fusion.18), kind=kOutput, calls=%fused_computation.18 | convolution fusion | flops 403079168 | bytes 7012352 | tf_op jit(solution)/shard_map/spcf,pfd->spcd/dot_general | solution.py:231
  255.6 1.9 copy.218
  257.5 4.4 %all-to-all-start.4 = ((bf16[32,2,2048]{2,1,0:T(2,128)(2,1)}), bf16[32,2,2048]{2,1,0:T(2,128)(2,1)}, u32[]{:S(2)}, u32[]{:S(2)}) async-start(bf16[32,2,2048]{2,1,0:T(2,128)(2,1)} %copy.218), calls=%async_computation.5 | async-start | bytes 524288 | tf_op jit(solution)/shard_map/all_to_all | solution.py:233
  261.9 0.7 and_select_fusion
  262.9 8.1 %all-to-all-done.4 = bf16[32,2,2048]{2,1,0:T(2,128)(2,1)} async-done(((bf16[32,2,2048]{2,1,0:T(2,128)(2,1)}), bf16[32,2,2048]{2,1,0:T(2,128)(2,1)}, u32[]{:S(2)}, u32[]{:S(2)}) %all-to-all-start.4) | async-done | bytes 262176 | tf_op jit(solution)/shard_map/all_to_all | solution.py:233
  271.0 2.0 convert_multiply_fusion
  273.0 2.2 reshape.325
  275.2 2.0 scatter_fusion
  277.2 0.7 convert_element_type.121
  (82 shorter events, 5.7 us)
Async XLA Ops:
  6.5 244.3 %copy-start = (bf16[1,768,2048]{2,1,0:T(8,128)(2,1)S(1)}, bf16[1,768,2048]{2,1,0:T(8,128)(2,1)}, u32[]{:S(2)}) copy-start(bf16[1,768,2048]{2,1,0:T(8,128)(2,1)} %param.32) | copy-start | bytes 9437188
  6.5 11.5 %copy-start.16 = (s32[1,8]{1,0:T(1,128)S(1)}, s32[1,8]{1,0:T(1,128)}, u32[]{:S(2)}) copy-start(s32[1,8]{1,0:T(1,128)} %param.37) | copy-start | bytes 100
  6.5 58.7 %copy-start.6 = (bf16[32,2048]{1,0:T(8,128)(2,1)S(1)}, bf16[32,2048]{1,0:T(8,128)(2,1)}, u32[]{:S(2)}) copy-start(bf16[32,2048]{1,0:T(8,128)(2,1)} %param.25) | copy-start | bytes 393220
  6.5 58.7 %all-gather.2.cloned.1.call-start = ((), (), s32[]{:S(2)}) async-start(), calls=%async_computation.6 | async-start | bytes 4325376 | tf_op jit(solution)/shard_map/all_gather | solution.py:181
  69.8 12.6 %all-to-all-start.1 = ((bf16[32,2,512]{2,1,0:T(2,128)(2,1)}), bf16[32,2,512]{2,1,0:T(2,128)(2,1)S(1)}, u32[]{:S(2)}, u32[]{:S(2)}) async-start(bf16[32,2,512]{2,1,0:T(2,128)(2,1)} %reshape.354), calls=%async_computation.1 | async-start | bytes 131072 | tf_op jit(solution)/shard_map/all_to_all | solution.py:188
  82.5 14.2 %all-to-all-start = ((bf16[32,32,128]{2,1,0:T(8,128)(2,1)}), bf16[32,32,128]{2,1,0:T(8,128)(2,1)S(1)}, u32[]{:S(2)}, u32[]{:S(2)}) async-start(bf16[32,32,128]{2,1,0:T(8,128)(2,1)} %bitcast.176), calls=%async_computation | async-start | bytes 524288 | tf_op jit(solution)/shard_map/all_to_all | solution.py:187
  86.8 138.5 %reduce-scatter.2.cloned.1.call-start = ((), (), s32[]{:S(2)}) async-start(), calls=%async_computation.7 | async-start | bytes 4325376 | tf_op jit(solution)/shard_map/reduce_scatter | solution.py:210
  98.7 4.8 %copy-start.10 = (pred[32,32]{0,1:T(8,128)(4,1)S(1)}, pred[32,32]{0,1:T(8,128)(4,1)}, u32[]{:S(2)}) copy-start(pred[32,32]{0,1:T(8,128)(4,1)} %copy.198) | copy-start | bytes 3076
  98.7 6.2 %copy-start.9 = (bf16[8,512]{1,0:T(8,128)(2,1)S(1)}, bf16[8,512]{1,0:T(8,128)(2,1)}, u32[]{:S(2)}) copy-start(bf16[8,512]{1,0:T(8,128)(2,1)} %gather_fusion.2) | copy-start | bytes 24580
  98.7 6.2 %copy-start.12 = (pred[8]{0:T(512)(128)(4,1)S(1)}, pred[8]{0:T(512)(128)(4,1)}, u32[]{:S(2)}) copy-start(pred[8]{0:T(512)(128)(4,1)} %get-tuple-element.32) | copy-start | bytes 28
  106.9 4.5 %copy-start.4 = (f32[4,8,32]{1,2,0:T(8,128)}, f32[4,8,32]{1,2,0:T(8,128)S(1)}, u32[]{:S(2)}) copy-start(f32[4,8,32]{1,2,0:T(8,128)S(1)} %copy.204) | copy-start | bytes 12292
  111.4 1.2 copy-start.5
  116.0 3.7 %copy-start.8 = (bf16[8,512]{1,0:T(8,128)(2,1)S(1)}, bf16[8,512]{1,0:T(8,128)(2,1)}, u32[]{:S(2)}) copy-start(bf16[8,512]{1,0:T(8,128)(2,1)} %gather_fusion.3) | copy-start | bytes 24580
  116.0 3.7 %copy-start.13 = (pred[8]{0:T(512)(128)(4,1)S(1)}, pred[8]{0:T(512)(128)(4,1)}, u32[]{:S(2)}) copy-start(pred[8]{0:T(512)(128)(4,1)} %get-tuple-element.32) | copy-start | bytes 28
  116.0 4.0 %copy-start.2 = (bf16[4,8,32,32]{3,1,2,0:T(8,128)(2,1)S(1)}, bf16[4,8,32,32]{3,1,2,0:T(8,128)(2,1)}, u32[]{:S(2)}) copy-start(bf16[4,8,32,32]{3,1,2,0:T(8,128)(2,1)} %copy.210) | copy-start | bytes 196612
  116.0 4.0 %copy-start.7 = (bf16[32,4,128]{2,1,0:T(4,128)(2,1)S(1)}, bf16[32,4,128]{2,1,0:T(4,128)(2,1)}, u32[]{:S(2)}) copy-start(bf16[32,4,128]{2,1,0:T(4,128)(2,1)} %reshape.282) | copy-start | bytes 98308
  119.7 16.9 %copy-start.3 = (bf16[128,2048]{1,0:T(8,128)(2,1)S(1)}, bf16[128,2048]{1,0:T(8,128)(2,1)}, u32[]{:S(2)}) copy-start(bf16[128,2048]{1,0:T(8,128)(2,1)} %param.28) | copy-start | bytes 1572868
  139.8 85.5 %copy-start.1 = (bf16[32,2048]{1,0:T(8,128)(2,1)S(1)}, bf16[32,2048]{1,0:T(8,128)(2,1)}, u32[]{:S(2)}) copy-start(bf16[32,2048]{1,0:T(8,128)(2,1)} %param.22) | copy-start | bytes 393220
  139.8 86.6 %copy-start.11 = (f32[2048]{0:T(1024)S(1)}, f32[2048]{0:T(1024)}, u32[]{:S(2)}) copy-start(f32[2048]{0:T(1024)} %param.29) | copy-start | bytes 24580
  141.6 84.8 %copy-start.15 = (s32[32,32]{0,1:T(8,128)}, s32[32,32]{0,1:T(8,128)S(1)}, u32[]{:S(2)}) copy-start(s32[32,32]{0,1:T(8,128)S(1)} %get-tuple-element.31) | copy-start | bytes 12292
  230.7 16.4 %all-to-all-start.3 = ((bf16[32,2,2048]{2,1,0:T(2,128)(2,1)}), bf16[32,2,2048]{2,1,0:T(2,128)(2,1)}, u32[]{:S(2)}, u32[]{:S(2)}) async-start(bf16[32,2,2048]{2,1,0:T(2,128)(2,1)} %reshape.308), calls=%async_computation.4 | async-start | bytes 524288 | tf_op jit(solution)/shard_map/all_to_all | solution.py:225
  250.8 11.8 %copy-start.14 = (s32[32,2]{0,1:T(2,128)S(1)}, s32[32,2]{0,1:T(2,128)}, u32[]{:S(2)}) copy-start(s32[32,2]{0,1:T(2,128)} %get-tuple-element.59) | copy-start | bytes 772
  257.5 13.5 %all-to-all-start.4 = ((bf16[32,2,2048]{2,1,0:T(2,128)(2,1)}), bf16[32,2,2048]{2,1,0:T(2,128)(2,1)}, u32[]{:S(2)}, u32[]{:S(2)}) async-start(bf16[32,2,2048]{2,1,0:T(2,128)(2,1)} %copy.218), calls=%async_computation.5 | async-start | bytes 524288 | tf_op jit(solution)/shard_map/all_to_all | solution.py:233
Sparse Core Ops, SparseCore 0:
  9.9 55.2 all-gather.1
  139.9 85.3 reduce-scatter.1
where the time goes:
time: 286 us; the launch traced here: 285 us
  waiting for transfers between devices  141 us (49%)
  local copies, waits for them, and re-layouts  32.4 us (11%)
  matrix products  31.7 us (11%)
  other arithmetic  26.5 us (9%)
  starting transfers between devices  21.3 us (7%)
  blocking collectives  16.2 us (6%)
  between operations  15.8 us (6%)
    reduce_scatter x1, waiting for transfers between devices, body(): lax.psum_scatter(jnp.dot(attn_heads, w_out, preferred_element_type=jnp.fl...  83 us
    all_gather x1, waiting for transfers between devices, body(): gathered = lax.all_gather(normed_own, 'tensor', axis=0, tiled=True)  40.2 us
    all_to_all x1, blocking collectives, body(): lax.all_to_all(attn_own, 'tensor', split_axis=1, concat_axis=0, tiled=True)  16.2 us
    all_to_all x1, waiting for transfers between devices, body(): lax.all_to_all(result.astype(jnp.bfloat16), 'tensor', split_axis=0, conca...  8.13 us
    all_to_all x1, starting transfers between devices, body(): lax.all_to_all(send_rows, 'tensor', split_axis=0, concat_axis=0, tiled=True)  7.32 us
    all_to_all x1, waiting for transfers between devices, body(): lax.all_to_all(send_rows, 'tensor', split_axis=0, concat_axis=0, tiled=True)  6.34 us
  transfers between devices with their start and end apart: 6, of which 5 were waited for; matrix products, arithmetic and copies ran while one was open for 12% of the time, Pallas kernels for 0%

commit v1 on v0

--- a/solution.py
+++ b/solution.py
@@ -178,7 +178,9 @@
     count_new = rows_here // slots_here
     row_start = own_index * rows_here
     normed_own = rms_rows(residual_in.astype(jnp.float32), attn_gain).astype(jnp.bfloat16)
-    gathered = lax.all_gather(normed_own, "tensor", axis=0, tiled=True)
+    gathered = jnp.concatenate(
+        lax.all_to_all(jnp.stack([normed_own] * lax.axis_size("tensor")), "tensor", 0, 0), axis=0
+    )
     query_part = jnp.dot(gathered, w_query, preferred_element_type=jnp.float32).astype(jnp.bfloat16)
     keyval_part = lax.dot_general(
         gathered, w_keyval, (((1,), (1,)), ((), ())), preferred_element_type=jnp.float32

time: 286 us -> 297 us (1.038)
  starting transfers between devices: 21.3 us -> 31.9 us
    all_gather x1 -> x0, waiting for transfers between devices: 40.2 us -> none  [body(): gathered = lax.all_gather(normed_own, 'tensor', axis=0, tiled=True)]
    all_to_all x0 -> x1, waiting for transfers between devices: none -> 37.3 us  [body(): lax.all_to_all(jnp.stack([normed_own] * lax.axis_size('tensor')), 'tensor...]
    all_to_all x0 -> x1, starting transfers between devices: none -> 8.78 us  [body(): lax.all_to_all(jnp.stack([normed_own] * lax.axis_size('tensor')), 'tensor...]
  transfers between devices with their start and end apart: 6 -> 6, of which waited for: 5 -> 5; matrix products, arithmetic and copies ran while one was open for 12% -> 11% of each run, Pallas kernels for 0% -> 0%
where the time goes in v1:
time: 297 us; the launch traced here: 295 us
  waiting for transfers between devices  139 us (47%)
  local copies, waits for them, and re-layouts  35 us (12%)
  starting transfers between devices  31.9 us (11%)
  matrix products  30.9 us (10%)
  other arithmetic  25.7 us (9%)
  blocking collectives  16.2 us (5%)
  between operations  15.9 us (5%)
    reduce_scatter x1, waiting for transfers between devices, body(): lax.psum_scatter(jnp.dot(attn_heads, w_out, preferred_element_type=jnp.fl...  84.5 us
    all_to_all x1, waiting for transfers between devices, body(): lax.all_to_all(jnp.stack([normed_own] * lax.axis_size('tensor')), 'tensor...  37.3 us
    all_to_all x1, blocking collectives, body(): lax.all_to_all(attn_own, 'tensor', split_axis=1, concat_axis=0, tiled=True)  16.2 us
    all_to_all x1, starting transfers between devices, body(): lax.all_to_all(jnp.stack([normed_own] * lax.axis_size('tensor')), 'tensor...  8.78 us
    all_to_all x1, waiting for transfers between devices, body(): lax.all_to_all(result.astype(jnp.bfloat16), 'tensor', split_axis=0, conca...  8.14 us
    all_to_all x1, starting transfers between devices, body(): lax.all_to_all(send_rows, 'tensor', split_axis=0, concat_axis=0, tiled=True)  7.3 us
    all_to_all x1, starting transfers between devices, body(): lax.all_to_all(keyval_part, 'tensor', split_axis=0, concat_axis=1, tiled=...  7.12 us
    all_to_all x1, waiting for transfers between devices, body(): lax.all_to_all(send_rows, 'tensor', split_axis=0, concat_axis=0, tiled=True)  6.34 us
  transfers between devices with their start and end apart: 6, of which 5 were waited for; matrix products, arithmetic and copies ran while one was open for 11% of the time, Pallas kernels for 0%

profile of v1, /device:TPU:1, one launch (start us, length us, event | category | flops | bytes accessed | tf_op | source)
XLA Modules:
  0.0 294.9 jit_solution(13470937600756113636)
XLA Ops:
  6.5 1.2 fusion.43
  7.7 1.0 fusion.45
  8.8 2.5 stack.2
  11.2 8.8 %all-to-all-start = ((bf16[32,32,2048]{2,1,0:T(8,128)(2,1)}), bf16[32,32,2048]{2,1,0:T(8,128)(2,1)}, u32[]{:S(2)}, u32[]{:S(2)}) async-start(bf16[32,32,2048]{2,1,0:T(8,128)(2,1)} %stack.2), calls=%async_computation | async-start | bytes 8388608 | tf_op jit(solution)/shard_map/all_to_all | solution.py:182
  23.0 0.7 copy.198
  23.7 2.1 reshape.282
  25.8 2.2 reshape.286
  28.6 2.5 gather_fusion.2
  31.1 2.5 gather_fusion.3
  34.2 0.7 multiply_cosine_fusion
  34.9 37.3 %all-to-all-done = bf16[32,32,2048]{2,1,0:T(8,128)(2,1)} async-done(((bf16[32,32,2048]{2,1,0:T(8,128)(2,1)}), bf16[32,32,2048]{2,1,0:T(8,128)(2,1)}, u32[]{:S(2)}, u32[]{:S(2)}) %all-to-all-start) | async-done | bytes 4194336 | tf_op jit(solution)/shard_map/all_to_all | solution.py:182
  72.3 3.5 %convolution_convert_fusion.2 = bf16[1024,32]{0,1:T(8,128)(2,1)S(1)} fusion(bf16[1024,2048]{1,0:T(8,128)(2,1)} %bitcast.2, bf16[32,2048]{1,0:T(8,128)(2,1)S(1)} %copy-done.6), kind=kOutput, calls=%fused_computation.38 | convolution fusion | flops 134250496 | bytes 4390912 | tf_op jit(solution)/shard_map/dot_general | solution.py:185
  76.0 0.9 reshape.360
  76.8 7.1 %all-to-all-start.2 = ((bf16[32,2,512]{2,1,0:T(2,128)(2,1)}), bf16[32,2,512]{2,1,0:T(2,128)(2,1)S(1)}, u32[]{:S(2)}, u32[]{:S(2)}) async-start(bf16[32,2,512]{2,1,0:T(2,128)(2,1)} %reshape.360), calls=%async_computation.2 | async-start | bytes 131072 | tf_op jit(solution)/shard_map/all_to_all | solution.py:190
  83.9 4.2 %convolution_convert_fusion.1 = bf16[1024,128]{1,0:T(8,128)(2,1)} fusion(bf16[1024,2048]{1,0:T(8,128)(2,1)} %bitcast.2, bf16[2048,128]{1,0:T(8,128)(2,1)} %param.24), kind=kOutput, calls=%fused_computation.29 | convolution fusion | flops 537001984 | bytes 4980736 | tf_op jit(solution)/shard_map/dot_general | solution.py:184
  88.2 3.1 %all-to-all-done.2 = bf16[32,2,512]{2,1,0:T(2,128)(2,1)S(1)} async-done(((bf16[32,2,512]{2,1,0:T(2,128)(2,1)}), bf16[32,2,512]{2,1,0:T(2,128)(2,1)S(1)}, u32[]{:S(2)}, u32[]{:S(2)}) %all-to-all-start.2) | async-done | bytes 65568 | tf_op jit(solution)/shard_map/all_to_all | solution.py:190
  91.3 4.3 %all-to-all-start.1 = ((bf16[32,32,128]{2,1,0:T(8,128)(2,1)}), bf16[32,32,128]{2,1,0:T(8,128)(2,1)S(1)}, u32[]{:S(2)}, u32[]{:S(2)}) async-start(bf16[32,32,128]{2,1,0:T(8,128)(2,1)} %bitcast.177), calls=%async_computation.1 | async-start | bytes 524288 | tf_op jit(solution)/shard_map/all_to_all | solution.py:189
  95.6 0.9 reshape.361
  96.5 1.8 copy.200
  98.3 1.2 squeeze.37
  100.2 0.9 reshape.296
  101.0 0.7 multiply_reduce_fusion.1
  101.7 0.8 copy.201
  102.5 0.7 fusion.62
  103.3 1.4 reshape.288
  104.7 0.8 subtract_convert_fusion.1
  105.7 0.9 fusion.41
  106.6 0.9 fusion.46
  107.7 4.0 %bitcast_reduce_fusion = (f32[4,8,32]{1,2,0:T(8,128)S(1)}, f32[4,32,8,1024]{3,2,1,0:T(8,128)}) fusion(pred[1024]{0:T(1024)(128)(4,1)} %fusion.79, bf16[1024,4,128,1]{2,1,0,3:T(4,128)(2,1)} %bitcast.169, bf16[32,4,8,128]{3,2,1,0:T(8,128)(2,1)S(1)} %pad_maximum_fusion), kind=kOutput, calls=%fused_computation.6 | convolution fusion | flops 271580160 | bytes 5510144 | tf_op jit(solution)/shard_map/while/body/eval_jaxpr/nkgd,mkd->kgnm/dot_general | solution.py:102
  111.7 0.7 copy.197
  112.4 1.3 fusion.91
  113.7 1.1 fusion.92
  114.8 0.7 maximum_maximum_fusion
  115.7 3.2 %fusion.1 = f32[4,8,32]{1,2,0:T(8,128)S(1)} fusion(f32[4,32,8,1024]{3,2,1,0:T(8,128)} %get-tuple-element.67, f32[4,8,32]{1,2,0:T(8,128)S(1)} %copy.204, pred[1024]{0:T(1024)(128)(4,1)} %fusion.79), kind=kLoop, calls=%fused_computation.11 | loop fusion | flops 4193280 | bytes 4203520 | tf_op jit(solution)/shard_map/while/body/eval_jaxpr/reduce_sum | solution.py:126
  119.0 1.2 fusion.42
  120.2 1.2 divide_convert_fusion.4
  122.0 0.8 copy.206
  122.8 0.9 copy.210
  123.7 1.0 copy.208
  124.7 3.7 %fusion.12 = f32[32,4,8,128]{3,2,0,1:T(8,128)S(1)} fusion(f32[4,32,8,1024]{3,2,1,0:T(8,128)} %get-tuple-element.67, f32[4,8,32]{1,2,0:T(8,128)S(1)} %copy.206, f32[4,8,32]{1,2,0:T(8,128)} %copy-done.4, pred[1024]{0:T(1024)(128)(4,1)} %fusion.79, bf16[1024,4,128,1]{2,1,0,3:T(4,128)(2,1)} %bitcast.175), kind=kOutput, calls=%fused_computation.20 | convolution fusion | flops 273678336 | bytes 5776384 | tf_op jit(solution)/shard_map/while/body/eval_jaxpr/kgnm,mkd->nkgd/dot_general | solution.py:133
  129.1 16.2 %all_to_all.60 = bf16[32,32,128]{2,0,1:T(8,128)(2,1)S(1)} all-to-all(bf16[32,32,128]{2,0,1:T(8,128)(2,1)S(1)} %copy.212), channel_id=1, replica_groups=mesh['group'=8,'tensor'=32] {'tensor'}, dimensions={1} | all-to-all | bytes 524288 | tf_op jit(solution)/shard_map/all_to_all | solution.py:211
  145.3 3.2 %convolution_convert_fusion = bf16[1024,2048]{1,0:T(8,128)(2,1)} fusion(bf16[1024,128]{1,0:T(8,128)(2,1)S(1)} %bitcast.170, bf16[128,2048]{1,0:T(8,128)(2,1)S(1)} %copy-done.3), kind=kOutput, calls=%fused_computation.10 | convolution fusion | flops 538968064 | bytes 4980736 | tf_op jit(solution)/shard_map/dot_general | solution.py:213
  148.5 0.8 constant_dynamic-slice_fusion.1
  149.5 0.8 sort.17
  151.0 84.5 %reduce-scatter.2.cloned.1.call-done = bf16[32,2048]{1,0:T(8,128)(2,1)} async-done(((bf16[1024,2048]{1,0:T(8,128)(2,1)}), bf16[32,2048]{1,0:T(8,128)(2,1)}) %reduce-scatter.2.cloned.1.call-update) | async-done | bytes 131088 | tf_op jit(solution)/shard_map/reduce_scatter | solution.py:212
  235.5 1.1 multiply_reduce_fusion
  236.6 1.1 multiply_convert_fusion
  237.7 1.4 gather_fusion
  239.1 1.8 reshape.314
  240.9 7.3 %all-to-all-start.4 = ((bf16[32,2,2048]{2,1,0:T(2,128)(2,1)}), bf16[32,2,2048]{2,1,0:T(2,128)(2,1)}, u32[]{:S(2)}, u32[]{:S(2)}) async-start(bf16[32,2,2048]{2,1,0:T(2,128)(2,1)} %reshape.314), calls=%async_computation.5 | async-start | bytes 524288 | tf_op jit(solution)/shard_map/all_to_all | solution.py:227
  248.2 0.7 bitcast_or_fusion
  249.1 0.8 constant_dynamic-slice_fusion
  249.9 0.8 gather_fusion.1
  250.9 6.3 %all-to-all-done.4 = bf16[32,2,2048]{2,1,0:T(2,128)(2,1)} async-done(((bf16[32,2,2048]{2,1,0:T(2,128)(2,1)}), bf16[32,2,2048]{2,1,0:T(2,128)(2,1)}, u32[]{:S(2)}, u32[]{:S(2)}) %all-to-all-start.4) | async-done | bytes 262176 | tf_op jit(solution)/shard_map/all_to_all | solution.py:227
  257.3 3.7 %fusion.18 = f32[32,1,2,768]{3,0,2,1:T(8,128)} fusion(bf16[1,768,2048]{2,1,0:T(8,128)(2,1)} %param.30, bf16[32,2,2048]{2,1,0:T(2,128)(2,1)} %all-to-all-done.4), kind=kOutput, calls=%fused_computation.30 | convolution fusion | flops 201326592 | bytes 3604480 | tf_op jit(solution)/shard_map/spcd,pfd->spcf/dot_general | solution.py:230
  261.0 4.8 %fusion.8 = bf16[32,2,2048]{2,0,1:T(8,128)(2,1)} fusion(bf16[1,768,2048]{2,1,0:T(8,128)(2,1)S(1)} %copy-done, bf16[1,768,2048]{2,1,0:T(8,128)(2,1)} %param.31, bf16[32,2,2048]{2,1,0:T(2,128)(2,1)} %all-to-all-done.4, f32[32,1,2,768]{3,0,2,1:T(8,128)} %fusion.18), kind=kOutput, calls=%fused_computation.18 | convolution fusion | flops 403079168 | bytes 7012352 | tf_op jit(solution)/shard_map/spcf,pfd->spcd/dot_general | solution.py:233
  265.8 1.9 copy.218
  267.7 4.4 %all-to-all-start.5 = ((bf16[32,2,2048]{2,1,0:T(2,128)(2,1)}), bf16[32,2,2048]{2,1,0:T(2,128)(2,1)}, u32[]{:S(2)}, u32[]{:S(2)}) async-start(bf16[32,2,2048]{2,1,0:T(2,128)(2,1)} %copy.218), calls=%async_computation.6 | async-start | bytes 524288 | tf_op jit(solution)/shard_map/all_to_all | solution.py:235
  272.1 0.7 and_select_fusion
  273.1 8.1 %all-to-all-done.5 = bf16[32,2,2048]{2,1,0:T(2,128)(2,1)} async-done(((bf16[32,2,2048]{2,1,0:T(2,128)(2,1)}), bf16[32,2,2048]{2,1,0:T(2,128)(2,1)}, u32[]{:S(2)}, u32[]{:S(2)}) %all-to-all-start.5) | async-done | bytes 262176 | tf_op jit(solution)/shard_map/all_to_all | solution.py:235
  281.2 2.0 convert_multiply_fusion
  283.2 2.2 reshape.331
  285.4 2.0 scatter_fusion
  287.4 0.7 convert_element_type.121
  (84 shorter events, 6.5 us)
Async XLA Ops:
  6.5 254.5 %copy-start = (bf16[1,768,2048]{2,1,0:T(8,128)(2,1)S(1)}, bf16[1,768,2048]{2,1,0:T(8,128)(2,1)}, u32[]{:S(2)}) copy-start(bf16[1,768,2048]{2,1,0:T(8,128)(2,1)} %param.32) | copy-start | bytes 9437188
  11.2 10.8 %copy-start.17 = (s32[1,32]{1,0:T(1,128)S(1)}, s32[1,32]{1,0:T(1,128)}, u32[]{:S(2)}) copy-start(s32[1,32]{1,0:T(1,128)} %param.38) | copy-start | bytes 388
  11.2 61.0 %all-to-all-start = ((bf16[32,32,2048]{2,1,0:T(8,128)(2,1)}), bf16[32,32,2048]{2,1,0:T(8,128)(2,1)}, u32[]{:S(2)}, u32[]{:S(2)}) async-start(bf16[32,32,2048]{2,1,0:T(8,128)(2,1)} %stack.2), calls=%async_computation | async-start | bytes 8388608 | tf_op jit(solution)/shard_map/all_to_all | solution.py:182
  20.0 8.0 %copy-start.16 = (s32[1,8]{1,0:T(1,128)S(1)}, s32[1,8]{1,0:T(1,128)}, u32[]{:S(2)}) copy-start(s32[1,8]{1,0:T(1,128)} %param.37) | copy-start | bytes 100
  20.0 52.2 %copy-start.6 = (bf16[32,2048]{1,0:T(8,128)(2,1)S(1)}, bf16[32,2048]{1,0:T(8,128)(2,1)}, u32[]{:S(2)}) copy-start(bf16[32,2048]{1,0:T(8,128)(2,1)} %param.25) | copy-start | bytes 393220
  76.8 14.5 %all-to-all-start.2 = ((bf16[32,2,512]{2,1,0:T(2,128)(2,1)}), bf16[32,2,512]{2,1,0:T(2,128)(2,1)S(1)}, u32[]{:S(2)}, u32[]{:S(2)}) async-start(bf16[32,2,512]{2,1,0:T(2,128)(2,1)} %reshape.360), calls=%async_computation.2 | async-start | bytes 131072 | tf_op jit(solution)/shard_map/all_to_all | solution.py:190
  91.3 14.2 %all-to-all-start.1 = ((bf16[32,32,128]{2,1,0:T(8,128)(2,1)}), bf16[32,32,128]{2,1,0:T(8,128)(2,1)S(1)}, u32[]{:S(2)}, u32[]{:S(2)}) async-start(bf16[32,32,128]{2,1,0:T(8,128)(2,1)} %bitcast.177), calls=%async_computation.1 | async-start | bytes 524288 | tf_op jit(solution)/shard_map/all_to_all | solution.py:189
  95.6 139.9 %reduce-scatter.2.cloned.1.call-start = ((), (), s32[]{:S(2)}) async-start(), calls=%async_computation.7 | async-start | bytes 4325376 | tf_op jit(solution)/shard_map/reduce_scatter | solution.py:212
  107.5 4.8 %copy-start.10 = (pred[32,32]{0,1:T(8,128)(4,1)S(1)}, pred[32,32]{0,1:T(8,128)(4,1)}, u32[]{:S(2)}) copy-start(pred[32,32]{0,1:T(8,128)(4,1)} %copy.198) | copy-start | bytes 3076
  107.6 6.2 %copy-start.9 = (bf16[8,512]{1,0:T(8,128)(2,1)S(1)}, bf16[8,512]{1,0:T(8,128)(2,1)}, u32[]{:S(2)}) copy-start(bf16[8,512]{1,0:T(8,128)(2,1)} %gather_fusion.2) | copy-start | bytes 24580
  107.6 6.2 %copy-start.12 = (pred[8]{0:T(512)(128)(4,1)S(1)}, pred[8]{0:T(512)(128)(4,1)}, u32[]{:S(2)}) copy-start(pred[8]{0:T(512)(128)(4,1)} %get-tuple-element.32) | copy-start | bytes 28
  115.6 4.5 %copy-start.4 = (f32[4,8,32]{1,2,0:T(8,128)}, f32[4,8,32]{1,2,0:T(8,128)S(1)}, u32[]{:S(2)}) copy-start(f32[4,8,32]{1,2,0:T(8,128)S(1)} %copy.204) | copy-start | bytes 12292
  120.2 1.2 copy-start.5
  124.7 3.7 %copy-start.8 = (bf16[8,512]{1,0:T(8,128)(2,1)S(1)}, bf16[8,512]{1,0:T(8,128)(2,1)}, u32[]{:S(2)}) copy-start(bf16[8,512]{1,0:T(8,128)(2,1)} %gather_fusion.3) | copy-start | bytes 24580
  124.7 3.7 %copy-start.13 = (pred[8]{0:T(512)(128)(4,1)S(1)}, pred[8]{0:T(512)(128)(4,1)}, u32[]{:S(2)}) copy-start(pred[8]{0:T(512)(128)(4,1)} %get-tuple-element.32) | copy-start | bytes 28
  124.7 4.0 %copy-start.2 = (bf16[4,8,32,32]{3,1,2,0:T(8,128)(2,1)S(1)}, bf16[4,8,32,32]{3,1,2,0:T(8,128)(2,1)}, u32[]{:S(2)}) copy-start(bf16[4,8,32,32]{3,1,2,0:T(8,128)(2,1)} %copy.210) | copy-start | bytes 196612
  124.7 4.0 %copy-start.7 = (bf16[32,4,128]{2,1,0:T(4,128)(2,1)S(1)}, bf16[32,4,128]{2,1,0:T(4,128)(2,1)}, u32[]{:S(2)}) copy-start(bf16[32,4,128]{2,1,0:T(4,128)(2,1)} %reshape.288) | copy-start | bytes 98308
  128.5 16.9 %copy-start.3 = (bf16[128,2048]{1,0:T(8,128)(2,1)S(1)}, bf16[128,2048]{1,0:T(8,128)(2,1)}, u32[]{:S(2)}) copy-start(bf16[128,2048]{1,0:T(8,128)(2,1)} %param.28) | copy-start | bytes 1572868
  148.5 87.0 %copy-start.1 = (bf16[32,2048]{1,0:T(8,128)(2,1)S(1)}, bf16[32,2048]{1,0:T(8,128)(2,1)}, u32[]{:S(2)}) copy-start(bf16[32,2048]{1,0:T(8,128)(2,1)} %param.22) | copy-start | bytes 393220
  148.5 88.1 %copy-start.11 = (f32[2048]{0:T(1024)S(1)}, f32[2048]{0:T(1024)}, u32[]{:S(2)}) copy-start(f32[2048]{0:T(1024)} %param.29) | copy-start | bytes 24580
  150.3 86.3 %copy-start.15 = (s32[32,32]{0,1:T(8,128)}, s32[32,32]{0,1:T(8,128)S(1)}, u32[]{:S(2)}) copy-start(s32[32,32]{0,1:T(8,128)S(1)} %get-tuple-element.31) | copy-start | bytes 12292
  240.9 16.3 %all-to-all-start.4 = ((bf16[32,2,2048]{2,1,0:T(2,128)(2,1)}), bf16[32,2,2048]{2,1,0:T(2,128)(2,1)}, u32[]{:S(2)}, u32[]{:S(2)}) async-start(bf16[32,2,2048]{2,1,0:T(2,128)(2,1)} %reshape.314), calls=%async_computation.5 | async-start | bytes 524288 | tf_op jit(solution)/shard_map/all_to_all | solution.py:227
  261.0 11.9 %copy-start.14 = (s32[32,2]{0,1:T(2,128)S(1)}, s32[32,2]{0,1:T(2,128)}, u32[]{:S(2)}) copy-start(s32[32,2]{0,1:T(2,128)} %get-tuple-element.59) | copy-start | bytes 772
  267.7 13.5 %all-to-all-start.5 = ((bf16[32,2,2048]{2,1,0:T(2,128)(2,1)}), bf16[32,2,2048]{2,1,0:T(2,128)(2,1)}, u32[]{:S(2)}, u32[]{:S(2)}) async-start(bf16[32,2,2048]{2,1,0:T(2,128)(2,1)} %copy.218), calls=%async_computation.6 | async-start | bytes 524288 | tf_op jit(solution)/shard_map/all_to_all | solution.py:235
Sparse Core Ops, SparseCore 0:
  148.6 86.8 reduce-scatter.1
